TPU v7x, 32 devices: a whole 2x2x4 slice. The times are simulated.
32 devices in a mesh: seq: 16 (over z, y, core), blk: 2 (over x).
Axes of the slice: x: 2, y: 2, z: 4, core: 2. Of those that a mesh axis runs over, the one named last changes fastest.
Arguments:
- tokens: bfloat16 [32, 1024, 512], P('seq', 'blk'), may hold values from -6 to 6
- memory: bfloat16 [32, 512, 512], P('seq', 'blk'), may hold values from -6 to 6
- segment_ends: int32 [32, 1024], P('seq', 'blk'), may hold values from 1 to 8192, as said below
- memory_ends: int32 [32, 512], P('seq', 'blk'), may hold values from -4088 to 0, as said below
- segment_counts: int32 [32], P('seq'), may hold values from 512 to 1024, as said below
- memory_lengths: int32 [32], P('seq'), may hold values from 128 to 512, as said below
- first_gain: float32 [512], replicated, may hold values from 0.5 to 1.5
- first_shift: float32 [512], replicated, may hold values from -1.2 to 1.2
- query_weight: bfloat16 [512, 512], replicated, may hold values from -0.25 to 0.25
- key_weight: bfloat16 [512, 512], replicated, may hold values from -0.25 to 0.25
- value_weight: bfloat16 [512, 512], replicated, may hold values from -0.25 to 0.25
- out_weight: bfloat16 [512, 512], replicated, may hold values from -2 to 2
- head_slopes: float32 [8], replicated, may hold values from 1e-05 to 0.03
- second_gain: float32 [512], replicated, may hold values from 0.5 to 1.5
- second_shift: float32 [512], replicated, may hold values from -1.2 to 1.2
- hidden_weight: bfloat16 [512, 2048], replicated, may hold values from -0.25 to 0.25
- output_weight: bfloat16 [2048, 512], replicated, may hold values from -0.125 to 0.125
- output_grad: bfloat16 [32, 1024, 512], P('seq', 'blk'), may hold values from -6 to 6
Outputs:
- layer_out: bfloat16 [32, 1024, 512], P('seq', 'blk')
- input_grad: bfloat16 [32, 1024, 512], P('seq', 'blk')
- grad_first_gain: float32 [512], replicated
- grad_first_shift: float32 [512], replicated
- grad_query_weight: float32 [512, 512], replicated
- grad_key_weight: float32 [512, 512], replicated
- grad_value_weight: float32 [512, 512], replicated
- grad_out_weight: float32 [512, 512], replicated
- grad_head_slopes: float32 [8], replicated
- grad_second_gain: float32 [512], replicated
- grad_second_shift: float32 [512], replicated
- grad_hidden_weight: float32 [512, 2048], replicated
- grad_output_weight: float32 [2048, 512], replicated
Inputs may be any that keep to these rules, and one draw needn't show every extreme that they name: `segment_ends`: each row rises strictly by 1 to 8 bytes from slot to slot; the first slot ends 1 to 8 bytes after the row's last memory end. In some sequence every step is 8 bytes; in another the first slot ends 1 byte after its memory. `memory_ends`: each row rises strictly by 1 to 8 bytes from entry to entry and its last entry is 0; in some sequence every step is 8 bytes. `segment_counts`: slots 0 to count - 1 of a sequence hold segments, the others are empty; some sequence uses all 1024 slots and some exactly half of them. `memory_lengths`: the last length memory rows of a sequence are valid; some sequence has all 512 and some a quarter.
All inputs are finite; a program needn't handle non-finite values.
Results may differ from a plain program's by a relative error of at most 0.022.
Values may be sent and summed in bfloat16 or wider, within the bound.
A program may use at most 256 MiB of HBM per device.

v0:
```python
import math
import jax
import jax.numpy as jnp
from jax import lax
from jax.sharding import PartitionSpec as P

epsilon = 1e-05
far_order = 1073741824


def layer_norm(values, gain, shift):
    centred = values - jnp.mean(values, axis=-1, keepdims=True)
    spread = jnp.mean(centred * centred, axis=-1, keepdims=True)
    return centred * lax.rsqrt(spread + epsilon) * gain + shift


def block_scores(
    q_heads, key_block, q_ends, key_order, key_ends, q_index, head_slopes, score_scale
):
    scores = (
        jnp.einsum("qhd,khd->hqk", q_heads, key_block, preferred_element_type=jnp.float32)
        * score_scale
    )
    distance = (q_ends[:, None] - key_ends[None, :]).astype(jnp.float32)
    scores = scores - head_slopes[:, None, None] * distance[None]
    allowed = key_order[None, :] <= q_index[:, None]
    return (jnp.where(allowed[None], scores, -1e30), distance)


def per_device(
    tokens,
    memory,
    segment_ends,
    memory_ends,
    segment_counts,
    memory_lengths,
    first_gain,
    first_shift,
    query_weight,
    key_weight,
    value_weight,
    out_weight,
    head_slopes,
    second_gain,
    second_shift,
    hidden_weight,
    output_weight,
    output_grad,
):
    seq_count, slot_count, model_width = tokens.shape
    mem_count = memory.shape[1]
    head_count = head_slopes.shape[0]
    head_dim = model_width // head_count
    score_scale = 1.0 / math.sqrt(head_dim)
    key_rows = mem_count + slot_count
    blocks = lax.axis_size("blk")
    my_block = lax.axis_index("blk")
    x_float = tokens.astype(jnp.float32)
    mem_float = memory.astype(jnp.float32)
    normed = layer_norm(x_float, first_gain, first_shift).astype(jnp.bfloat16)
    mem_normed = layer_norm(mem_float, first_gain, first_shift).astype(jnp.bfloat16)
    key_input = jnp.concatenate([mem_normed, normed], axis=1)
    query = jnp.einsum(
        "std,de->ste", normed, query_weight, preferred_element_type=jnp.float32
    ).astype(jnp.bfloat16)
    pair_weight = jnp.concatenate([key_weight, value_weight], axis=1)
    key_value = jnp.einsum(
        "srd,de->rse", key_input, pair_weight, preferred_element_type=jnp.float32
    ).astype(jnp.bfloat16)
    mem_index = my_block * mem_count + jnp.arange(mem_count, dtype=jnp.int32)
    slot_index = my_block * slot_count + jnp.arange(slot_count, dtype=jnp.int32)
    mem_order = jnp.where(
        mem_index[None, :] >= mem_count * blocks - memory_lengths[:, None], -1, far_order
    )
    slot_order = jnp.where(
        slot_index[None, :] < segment_counts[:, None], slot_index[None, :], far_order
    )
    key_meta = jnp.stack(
        [
            jnp.concatenate([mem_order, slot_order], axis=1),
            jnp.concatenate([memory_ends, segment_ends], axis=1),
        ]
    )
    all_pairs, all_meta = (
        lax.all_gather(key_value, "blk", axis=0, tiled=True),
        lax.all_gather(key_meta, "blk", axis=2, tiled=True),
    )
    query_heads = query.reshape(seq_count, slot_count, head_count, head_dim)

    def pick(seq_index):
        pair_rows = lax.dynamic_index_in_dim(all_pairs, seq_index, 1, keepdims=False)
        meta_rows = lax.dynamic_index_in_dim(all_meta, seq_index, 1, keepdims=False)
        key_heads = pair_rows[:, :model_width].reshape(-1, key_rows, head_count, head_dim)
        value_heads = pair_rows[:, model_width:].reshape(-1, key_rows, head_count, head_dim)
        return (
            key_heads,
            value_heads,
            meta_rows[0].reshape(-1, key_rows),
            meta_rows[1].reshape(-1, key_rows),
        )

    def attend(seq_index):
        key_heads, value_heads, key_order, key_ends = pick(seq_index)
        q_heads = lax.dynamic_index_in_dim(query_heads, seq_index, 0, keepdims=False)
        q_ends = lax.dynamic_index_in_dim(segment_ends, seq_index, 0, keepdims=False)

        def stats_step(running, pieces):
            scores = block_scores(
                q_heads,
                pieces[0],
                q_ends,
                pieces[1],
                pieces[2],
                slot_index,
                head_slopes,
                score_scale,
            )[0]
            running_max = jnp.maximum(running[0], jnp.max(scores, axis=-1))
            running_sum = running[1] * jnp.exp(running[0] - running_max) + jnp.sum(
                jnp.exp(scores - running_max[..., None]), axis=-1
            )
            return ((running_max, running_sum), None)

        start_max = jnp.full((head_count, slot_count), -jnp.inf, jnp.float32)
        (top_max, top_sum), _ = lax.scan(
            stats_step, (start_max, jnp.zeros_like(start_max)), (key_heads, key_order, key_ends)
        )
        log_total = top_max + jnp.log(top_sum)

        def out_step(summed, pieces):
            scores = block_scores(
                q_heads,
                pieces[0],
                q_ends,
                pieces[1],
                pieces[2],
                slot_index,
                head_slopes,
                score_scale,
            )[0]
            attn_probs = jnp.exp(scores - log_total[..., None]).astype(jnp.bfloat16)
            return (
                summed
                + jnp.einsum(
                    "hqk,khd->qhd", attn_probs, pieces[3], preferred_element_type=jnp.float32
                ),
                None,
            )

        start_out = jnp.zeros((slot_count, head_count, head_dim), jnp.float32)
        mixed_heads, _ = lax.scan(
            out_step, start_out, (key_heads, key_order, key_ends, value_heads)
        )
        return (mixed_heads, log_total)

    mixed_all, log_totals = lax.map(attend, jnp.arange(seq_count))
    mixed_low = mixed_all.reshape(seq_count, slot_count, model_width).astype(jnp.bfloat16)
    residual = x_float + jnp.einsum(
        "std,de->ste", mixed_low, out_weight, preferred_element_type=jnp.float32
    )
    second_low = layer_norm(residual, second_gain, second_shift).astype(jnp.bfloat16)
    hidden_pre = jnp.einsum(
        "std,df->stf", second_low, hidden_weight, preferred_element_type=jnp.float32
    )
    act_low = jax.nn.gelu(hidden_pre, approximate=False).astype(jnp.bfloat16)
    layer_out = (
        residual
        + jnp.einsum("stf,fd->std", act_low, output_weight, preferred_element_type=jnp.float32)
    ).astype(jnp.bfloat16)
    grad_output_w = jnp.einsum(
        "stf,std->fd", act_low, output_grad, preferred_element_type=jnp.float32
    )
    d_act = jnp.einsum(
        "std,fd->stf", output_grad, output_weight, preferred_element_type=jnp.float32
    )
    _, gelu_pull = jax.vjp(lambda inner: jax.nn.gelu(inner, approximate=False), hidden_pre)
    d_pre_low = gelu_pull(d_act)[0].astype(jnp.bfloat16)
    grad_hidden_w = jnp.einsum(
        "std,stf->df", second_low, d_pre_low, preferred_element_type=jnp.float32
    )
    d_second = jnp.einsum(
        "stf,df->std", d_pre_low, hidden_weight, preferred_element_type=jnp.float32
    )
    _, second_pull = jax.vjp(layer_norm, residual, second_gain, second_shift)
    d_resid_norm, grad_second_g, grad_second_b = second_pull(d_second)
    d_residual = d_resid_norm + output_grad.astype(jnp.float32)
    d_branch = d_residual.astype(jnp.bfloat16)
    grad_out_w = jnp.einsum("std,ste->de", mixed_low, d_branch, preferred_element_type=jnp.float32)
    d_mixed = jnp.einsum(
        "ste,de->std", d_branch, out_weight, preferred_element_type=jnp.float32
    ).astype(jnp.bfloat16)
    d_mixed_heads = d_mixed.reshape(seq_count, slot_count, head_count, head_dim)

    def query_side(seq_index):
        key_heads, value_heads, key_order, key_ends = pick(seq_index)
        q_heads = lax.dynamic_index_in_dim(query_heads, seq_index, 0, keepdims=False)
        q_ends = lax.dynamic_index_in_dim(segment_ends, seq_index, 0, keepdims=False)
        d_heads = lax.dynamic_index_in_dim(d_mixed_heads, seq_index, 0, keepdims=False)
        log_total = lax.dynamic_index_in_dim(log_totals, seq_index, 0, keepdims=False)

        def probs_of(key_block, order_block, ends_block, value_block):
            scores, distance = block_scores(
                q_heads,
                key_block,
                q_ends,
                order_block,
                ends_block,
                slot_index,
                head_slopes,
                score_scale,
            )
            attn_probs = jnp.exp(scores - log_total[..., None])
            d_probs = jnp.einsum(
                "qhd,khd->hqk", d_heads, value_block, preferred_element_type=jnp.float32
            )
            return (attn_probs, d_probs, distance)

        def delta_step(summed, pieces):
            attn_probs, d_probs, _ = probs_of(pieces[0], pieces[1], pieces[2], pieces[3])
            return (summed + jnp.sum(attn_probs * d_probs, axis=-1), None)

        delta_rows, _ = lax.scan(
            delta_step,
            jnp.zeros((head_count, slot_count), jnp.float32),
            (key_heads, key_order, key_ends, value_heads),
        )

        def grad_step(running, pieces):
            attn_probs, d_probs, distance = probs_of(pieces[0], pieces[1], pieces[2], pieces[3])
            d_scores = (attn_probs * (d_probs - delta_rows[..., None])).astype(jnp.bfloat16)
            d_query = running[0] + jnp.einsum(
                "hqk,khd->qhd", d_scores, pieces[0], preferred_element_type=jnp.float32
            )
            d_slopes = running[1] - jnp.sum(
                d_scores.astype(jnp.float32) * distance[None], axis=(1, 2)
            )
            return ((d_query, d_slopes), None)

        start_grads = (
            jnp.zeros((slot_count, head_count, head_dim), jnp.float32),
            jnp.zeros((head_count,), jnp.float32),
        )
        (d_query, d_slopes), _ = lax.scan(
            grad_step, start_grads, (key_heads, key_order, key_ends, value_heads)
        )
        return (d_query * score_scale, delta_rows, d_slopes)

    d_query_all, delta_all, slope_parts = lax.map(query_side, jnp.arange(seq_count))
    grad_slopes = jnp.sum(slope_parts, axis=0)
    d_query_low = d_query_all.reshape(seq_count, slot_count, model_width).astype(jnp.bfloat16)

    def pair_terms(
        pair_rows, order_block, ends_block, q_heads, q_ends, q_index, d_heads, log_total, delta_rows
    ):
        key_block = pair_rows[:, :model_width].reshape(key_rows, head_count, head_dim)
        value_block = pair_rows[:, model_width:].reshape(key_rows, head_count, head_dim)
        scores, _ = block_scores(
            q_heads, key_block, q_ends, order_block, ends_block, q_index, head_slopes, score_scale
        )
        attn_probs = jnp.exp(scores - log_total[..., None])
        d_probs = jnp.einsum(
            "qhd,khd->hqk", d_heads, value_block, preferred_element_type=jnp.float32
        )
        d_scores = (attn_probs * (d_probs - delta_rows[..., None])).astype(jnp.bfloat16)
        d_value = jnp.einsum(
            "hqk,qhd->khd",
            attn_probs.astype(jnp.bfloat16),
            d_heads,
            preferred_element_type=jnp.float32,
        )
        d_key = (
            jnp.einsum("hqk,qhd->khd", d_scores, q_heads, preferred_element_type=jnp.float32)
            * score_scale
        )
        return jnp.concatenate(
            [d_key.reshape(key_rows, model_width), d_value.reshape(key_rows, model_width)], axis=1
        )

    def one_block(block_index):
        offset = block_index * key_rows
        pair_block = lax.dynamic_slice_in_dim(all_pairs, offset, key_rows, 0)
        meta_block = lax.dynamic_slice_in_dim(all_meta, offset, key_rows, 2)
        return jax.vmap(pair_terms, in_axes=(1, 0, 0, 0, 0, None, 0, 0, 0), out_axes=1)(
            pair_block,
            meta_block[0],
            meta_block[1],
            query_heads,
            segment_ends,
            slot_index,
            d_mixed_heads,
            log_totals,
            delta_all,
        )

    pieces = lax.map(one_block, jnp.arange(lax.axis_size("blk") * key_rows // key_rows))
    pair_grads = lax.psum_scatter(
        pieces.reshape(lax.axis_size("blk") * key_rows, seq_count, 2 * model_width).astype(
            jnp.bfloat16
        ),
        "blk",
        scatter_dimension=0,
        tiled=True,
    )
    grad_pair_w = jnp.einsum(
        "srd,rse->de", key_input, pair_grads, preferred_element_type=jnp.float32
    )
    grad_key_w = grad_pair_w[:, :model_width]
    grad_value_w = grad_pair_w[:, model_width:]
    d_key_input = jnp.einsum(
        "rse,de->srd", pair_grads, pair_weight, preferred_element_type=jnp.float32
    )
    grad_query_w = jnp.einsum(
        "std,ste->de", normed, d_query_low, preferred_element_type=jnp.float32
    )
    d_normed = (
        jnp.einsum("ste,de->std", d_query_low, query_weight, preferred_element_type=jnp.float32)
        + d_key_input[:, mem_count:]
    )
    _, first_pull = jax.vjp(layer_norm, x_float, first_gain, first_shift)
    d_tokens, gain_slots, shift_slots = first_pull(d_normed)
    _, mem_pull = jax.vjp(
        lambda gain, shift: layer_norm(mem_float, gain, shift), first_gain, first_shift
    )
    gain_mem, shift_mem = mem_pull(d_key_input[:, :mem_count])
    input_grad = (d_tokens + d_residual).astype(jnp.bfloat16)
    grad_first_g = gain_slots + gain_mem
    grad_first_b = shift_slots + shift_mem
    summed = lax.psum(
        (
            grad_first_g,
            grad_first_b,
            grad_query_w,
            grad_key_w,
            grad_value_w,
            grad_out_w,
            grad_slopes,
            grad_second_g,
            grad_second_b,
            grad_hidden_w,
            grad_output_w,
        ),
        ("seq", "blk"),
    )
    return (
        layer_out,
        input_grad,
        summed[0],
        summed[1],
        summed[2],
        summed[3],
        summed[4],
        summed[5],
        summed[6],
        summed[7],
        summed[8],
        summed[9],
        summed[10],
    )


def solution(mesh):
    placed = (
        P("seq", "blk", None),
        P("seq", "blk", None),
        P("seq", "blk"),
        P("seq", "blk"),
        P("seq"),
        P("seq"),
        P(),
        P(),
        P(),
        P(),
        P(),
        P(),
        P(),
        P(),
        P(),
        P(),
        P(),
        P("seq", "blk", None),
    )
    return jax.shard_map(
        per_device,
        mesh=mesh,
        in_specs=placed,
        out_specs=(
            P("seq", "blk", None),
            P("seq", "blk", None),
            P(),
            P(),
            P(),
            P(),
            P(),
            P(),
            P(),
            P(),
            P(),
            P(),
            P(),
        ),
        check_vma=False,
    )
```

profile of v0, /device:TPU:0, one launch (start us, length us, event | category | flops | bytes accessed | tf_op | source)
XLA Modules:
  0.0 937.2 jit_solution(17816046465124142338)
XLA Ops:
  26.0 5.4 all_gather.7
  34.2 73.6 %all-gather.2.cloned.1.call-done = bf16[1536,2,1024]{0,2,1:T(8,128)(2,1)} async-done(((bf16[768,2,1024]{0,2,1:T(8,128)(2,1)}), bf16[1536,2,1024]{0,2,1:T(8,128)(2,1)}) %all-gather.2.cloned.1.call-update) | async-done | bytes 6291472 | tf_op jit(solution)/shard_map/all_gather | solution.py:85
  110.0 168.7 %while.93 = (s32[]{:T(128)}, bf16[2,512,8,64]{1,3,2,0:T(8,128)(2,1)}, f32[2,8,512]{2,1,0:T(8,128)}, s32[2]{0:T(128)}, bf16[1536,2,1024]{0,2,1:T(8,128)(2,1)}, /*...) while((s32[]{:T(128)}, ...), condition=%wide.region_11.12_spmd.clone, body=%wide.region_4.11_spmd.clone.sunk | while | flops 1264345600 | bytes 82579288 | solution.py:156
  123.6 4.6 reshape.453
  131.0 4.6 reshape.454
  138.4 21.8 %while.98 = (s32[]{:T(128)}, f32[8,512]{1,0:T(8,128)S(1)}, f32[8,512]{1,0:T(8,128)S(1)}, s32[2,768]{1,0:T(2,128)S(1)}, s32[512]{0:T(512)S(1)}, /*index=5*/bf16[2...) while((s32[]{:T(128)}, f32[8,512]{1,0:T(8,128)S(1)}, ...), condition=%wide.region_8.8_spmd.clone, body=%wide.region_5.7_spmd.clone.sunk | while | flops 438456320 | bytes 32610988 | solution.py:125
  139.6 5.3 fusion.232
  145.0 4.3 exponential_reduce_fusion.2
  150.5 5.3 fusion.232
  155.9 4.3 exponential_reduce_fusion.2
  160.9 31.5 %while.99 = (s32[]{:T(128)}, f32[512,8,64]{0,2,1:T(8,128)}, bf16[2,768,8,64]{1,3,2,0:T(8,128)(2,1)}, s32[2,768]{1,0:T(2,128)S(1)}, s32[512]{0:T(512)S(1)}, /*ind...) while((s32[]{:T(128)}, f32[512,8,64]{0,2,1:T(8,128)}, ...), condition=%wide.region_10.10_spmd.clone, body=%wide.region_9.9_spmd.clone.sunk | while | flops 825884672 | bytes 19438292 | solution.py:151
  163.3 4.3 constant_dynamic-slice_fusion.18
  167.6 8.0 fusion.238
  179.0 4.3 constant_dynamic-slice_fusion.18
  183.4 8.1 fusion.238
  207.6 4.6 reshape.453
  215.0 4.6 reshape.454
  222.5 21.8 %while.98 = (s32[]{:T(128)}, f32[8,512]{1,0:T(8,128)S(1)}, f32[8,512]{1,0:T(8,128)S(1)}, s32[2,768]{1,0:T(2,128)S(1)}, s32[512]{0:T(512)S(1)}, /*index=5*/bf16[2...) while((s32[]{:T(128)}, f32[8,512]{1,0:T(8,128)S(1)}, ...), condition=%wide.region_8.8_spmd.clone, body=%wide.region_5.7_spmd.clone.sunk | while | flops 438456320 | bytes 32610988 | solution.py:125
  223.7 5.3 fusion.232
  229.0 4.3 exponential_reduce_fusion.2
  234.5 5.3 fusion.232
  239.9 4.3 exponential_reduce_fusion.2
  244.9 31.5 %while.99 = (s32[]{:T(128)}, f32[512,8,64]{0,2,1:T(8,128)}, bf16[2,768,8,64]{1,3,2,0:T(8,128)(2,1)}, s32[2,768]{1,0:T(2,128)S(1)}, s32[512]{0:T(512)S(1)}, /*ind...) while((s32[]{:T(128)}, f32[512,8,64]{0,2,1:T(8,128)}, ...), condition=%wide.region_10.10_spmd.clone, body=%wide.region_9.9_spmd.clone.sunk | while | flops 825884672 | bytes 19438292 | solution.py:151
  247.3 4.3 constant_dynamic-slice_fusion.18
  251.6 8.1 fusion.238
  263.1 4.3 constant_dynamic-slice_fusion.18
  267.4 8.1 fusion.238
  281.7 4.2 fusion.108
  286.0 20.1 %multiply_convert_fusion = (bf16[2,512,2048]{2,1,0:T(8,128)(2,1)}, f32[2,512,2048]{2,1,0:T(8,128)}) fusion(f32[2,512,2048]{2,1,0:T(8,128)S(1)} %get-tuple-element.1058, u8[512,2048]{1,0:T(8,128)(4,1)S(1)} %get-tuple-element.841, u8[512,2048]{1,0:T(8,128)(4,1)S(1)} %get-tuple-element.840), kind=kLoop, calls=%fused_computation.134 | loop fusion | flops 146800640 | bytes 23068672 | tf_op jit(solution)/shard_map/convert_element_type | solution.py:165
  306.1 6.8 add_convert_fusion
  322.6 155.2 %while.96 = (s32[]{:T(128)}, bf16[2,512,8,64]{1,3,2,0:T(8,128)(2,1)}, f32[2,8,512]{2,1,0:T(8,128)}, f32[2,8]{1,0:T(2,128)}, s32[2]{0:T(128)}, /*index=5*/bf16[15...) while((s32[]{:T(128)}, ...), condition=%wide.region_23.24_spmd.clone, body=%wide.region_16.23_spmd.clone.sunk | while | flops 2073039360 | bytes 125587736 | solution.py:248
  334.2 4.7 copy.151
  348.6 5.2 reshape.456
  353.7 4.4 copy.153
  358.2 18.1 %while.100 = (s32[]{:T(128)}, f32[8,512]{1,0:T(8,128)S(1)}, s32[2,768]{1,0:T(2,128)S(1)}, s32[512]{0:T(512)S(1)}, bf16[2,768,8,64]{1,3,2,0:T(8,128)(2,1)S(1)}, /...) while((s32[]{:T(128)}, f32[8,512]{1,0:T(8,128)S(1)}, ...), condition=%wide.region_19.19_spmd.clone, body=%wide.region_17.18_spmd.clone.sunk | while | flops 828510208 | bytes 40212728 | solution.py:222
  360.5 6.6 fusion.222
  369.6 6.6 fusion.222
  376.3 23.0 %while.101 = (s32[]{:T(128)}, f32[512,8,64]{0,2,1:T(8,128)S(1)}, f32[8]{0:T(128)S(1)}, bf16[2,768,8,64]{1,3,2,0:T(8,128)(2,1)S(1)}, s32[2,768]{1,0:T(2,128)S(1)}...) while((s32[]{:T(128)}, f32[512,8,64]{0,2,1:T(8,128)S(1)}, ...), condition=%wide.region_22.22_spmd.clone, body=%wide.region_20.21_spmd.clone.sunk | while | flops 1244266496 | bytes 49339216 | solution.py:243
  378.6 7.8 multiply_reduce_fusion.5
  390.1 7.8 multiply_reduce_fusion.5
  407.8 3.8 constant_dynamic-slice_fusion.15
  411.6 4.7 copy.151
  425.9 5.2 reshape.456
  431.1 4.4 copy.153
  435.5 18.1 %while.100 = (s32[]{:T(128)}, f32[8,512]{1,0:T(8,128)S(1)}, s32[2,768]{1,0:T(2,128)S(1)}, s32[512]{0:T(512)S(1)}, bf16[2,768,8,64]{1,3,2,0:T(8,128)(2,1)S(1)}, /...) while((s32[]{:T(128)}, f32[8,512]{1,0:T(8,128)S(1)}, ...), condition=%wide.region_19.19_spmd.clone, body=%wide.region_17.18_spmd.clone.sunk | while | flops 828510208 | bytes 40212728 | solution.py:222
  437.9 6.6 fusion.222
  446.9 6.6 fusion.222
  453.6 23.0 %while.101 = (s32[]{:T(128)}, f32[512,8,64]{0,2,1:T(8,128)S(1)}, f32[8]{0:T(128)S(1)}, bf16[2,768,8,64]{1,3,2,0:T(8,128)(2,1)S(1)}, s32[2,768]{1,0:T(2,128)S(1)}...) while((s32[]{:T(128)}, f32[512,8,64]{0,2,1:T(8,128)S(1)}, ...), condition=%wide.region_22.22_spmd.clone, body=%wide.region_20.21_spmd.clone.sunk | while | flops 1244266496 | bytes 49339216 | solution.py:243
  456.0 7.8 multiply_reduce_fusion.5
  467.5 7.8 multiply_reduce_fusion.5
  477.8 116.6 %while.97 = (s32[]{:T(128)}, bf16[2,768,2,1024]{3,1,0,2:T(8,128)(2,1)}, s32[2]{0:T(128)S(1)}, s32[2,2,1536]{2,1,0:T(2,128)}, bf16[1536,2,1024]{0,2,1:T(8,128)(2,...) while((s32[]{:T(128)}, ...), condition=%wide.region_25.26_spmd.clone, body=%wide.region_24.25_spmd.clone.sunk | while | flops 3319529984 | bytes 129511832 | solution.py:295
  485.4 11.3 %fusion.214 = f32[2,8,768,512]{3,2,1,0:T(8,128)} fusion(bf16[2,768,8,64]{1,3,2,0:T(8,128)(2,1)S(1)} %bitcast.354, bf16[2,512,8,64]{1,3,2,0:T(8,128)(2,1)} %get-tuple-element.2049), kind=kOutput, calls=%fused_computation.237.clone.1 | convolution fusion | flops 805306368 | bytes 27787264 | tf_op jit(solution)/shard_map/while/body/eval_jaxpr/vmap(qhd,khd->hqk)/dot_general | solution.py:21
  496.8 19.0 %fusion.216 = bf16[2,8,768,64]{2,3,1,0:T(8,128)(2,1)} fusion(bf16[2,512,8,64]{1,3,2,0:T(8,128)(2,1)} %get-tuple-element.2049, f32[2,8,768,512]{3,2,1,0:T(8,128)} %fusion.214, f32[2,8,512]{2,1,0:T(8,128)S(1)} %copy-done.60, f32[2,8,512]{2,1,0:T(8,128)} %get-tuple-element.2052, f32[2,512,768]{1,2,0:T(8,128)S(1)} %subtract_convert_fusion.10, ...), kind=kOutput, calls=%fused_computation.15.clone.1 | convolution fusion | flops 1662517248 | bytes 34406432 | tf_op jit(solution)/shard_map/while/body/eval_jaxpr/vmap(hqk,qhd->khd)/dot_general | solution.py:272
  515.8 13.2 %fusion.215 = bf16[2,8,768,64]{2,3,1,0:T(8,128)(2,1)S(1)} fusion(bf16[2,512,8,64]{1,3,2,0:T(8,128)(2,1)} %get-tuple-element.2053, f32[2,8,768,512]{3,2,1,0:T(8,128)} %fusion.214, f32[2,8,512]{2,1,0:T(8,128)} %get-tuple-element.2052, f32[2,512,768]{1,2,0:T(8,128)S(1)} %subtract_convert_fusion.10, f32[8]{0:T(128)} %get-tuple-element.2050, ...), kind=kOutput, calls=%fused_computation.10.clone.1 | convolution fusion | flops 843055104 | bytes 31752224 | tf_op jit(solution)/shard_map/while/body/eval_jaxpr/vmap(hqk,qhd->khd)/dot_general | solution.py:265
  543.7 11.3 %fusion.214 = f32[2,8,768,512]{3,2,1,0:T(8,128)} fusion(bf16[2,768,8,64]{1,3,2,0:T(8,128)(2,1)S(1)} %bitcast.354, bf16[2,512,8,64]{1,3,2,0:T(8,128)(2,1)} %get-tuple-element.2049), kind=kOutput, calls=%fused_computation.237.clone.1 | convolution fusion | flops 805306368 | bytes 27787264 | tf_op jit(solution)/shard_map/while/body/eval_jaxpr/vmap(qhd,khd->hqk)/dot_general | solution.py:21
  555.0 19.0 %fusion.216 = bf16[2,8,768,64]{2,3,1,0:T(8,128)(2,1)} fusion(bf16[2,512,8,64]{1,3,2,0:T(8,128)(2,1)} %get-tuple-element.2049, f32[2,8,768,512]{3,2,1,0:T(8,128)} %fusion.214, f32[2,8,512]{2,1,0:T(8,128)S(1)} %copy-done.60, f32[2,8,512]{2,1,0:T(8,128)} %get-tuple-element.2052, f32[2,512,768]{1,2,0:T(8,128)S(1)} %subtract_convert_fusion.10, ...), kind=kOutput, calls=%fused_computation.15.clone.1 | convolution fusion | flops 1662517248 | bytes 34406432 | tf_op jit(solution)/shard_map/while/body/eval_jaxpr/vmap(hqk,qhd->khd)/dot_general | solution.py:272
  574.0 13.2 %fusion.215 = bf16[2,8,768,64]{2,3,1,0:T(8,128)(2,1)S(1)} fusion(bf16[2,512,8,64]{1,3,2,0:T(8,128)(2,1)} %get-tuple-element.2053, f32[2,8,768,512]{3,2,1,0:T(8,128)} %fusion.214, f32[2,8,512]{2,1,0:T(8,128)} %get-tuple-element.2052, f32[2,512,768]{1,2,0:T(8,128)S(1)} %subtract_convert_fusion.10, f32[8]{0:T(128)} %get-tuple-element.2050, ...), kind=kOutput, calls=%fused_computation.10.clone.1 | convolution fusion | flops 843055104 | bytes 31752224 | tf_op jit(solution)/shard_map/while/body/eval_jaxpr/vmap(hqk,qhd->khd)/dot_general | solution.py:265
  600.9 4.4 convolution_bitcast_fusion.1
  605.4 4.7 convolution_bitcast_fusion.2
  610.0 61.7 %reduce-scatter.2.cloned.1.call-done = bf16[768,2,1024]{2,0,1:T(8,128)(2,1)} async-done(((bf16[1536,2,1024]{2,0,1:T(8,128)(2,1)}), bf16[768,2,1024]{2,0,1:T(8,128)(2,1)}) %reduce-scatter.2.cloned.1.call-update) | async-done | bytes 3145744 | tf_op jit(solution)/shard_map/reduce_scatter | solution.py:296
  671.7 4.2 convolution_bitcast_fusion.4
  678.1 6.3 add_convert_fusion.2
  690.5 41.0 %all-reduce = (f32[512]{0:T(512)}, f32[512]{0:T(512)}, f32[8]{0:T(128)}, f32[512]{0:T(512)}, f32[512]{0:T(512)}) all-reduce(f32[512]{0:T(512)S(1)} %add.197, f32[512]{0:T(512)S(1)} %add.198, f32[8]{0:T(128)S(1)} %reduce_sum.201, f32[512]{0:T(512)S(1)} %copy-done.65, ...), channel_id=1, replica_groups=mesh['seq'=16,'blk'=2] {'seq','blk'}, use_global_device_ids=true, to_apply=%region_31.32 | all-reduce | flops 2056 | bytes 16448 | tf_op jit(solution)/shard_map/psum | solution.py:328
  734.8 183.1 %all-reduce.4.cloned.1.call-done = (f32[512,512]{1,0:T(8,128)}, f32[512,512]{1,0:T(8,128)}, f32[512,512]{1,0:T(8,128)}, f32[512,512]{1,0:T(8,128)}, f32[512,2048]{1,0:T(8,128)}, /*index=5*/f32[2048,512]{1,0:T(8,128)}) async-done(((f32[512,512]{1,0:T(8,128)}, f32[512,512]{1,0:T(8,128)}, f32[512,512]{1,0:T(8,128)}, f32[512,512]{1,0:T(8,128)}, f32[512,2048]{1,0:T(8,128)}, /*index=5*/f32[2048,512]{1,0:T(8,128)}), ...) | async-done | bytes 12582928 | tf_op jit(solution)/shard_map/psum | solution.py:328
  (424 shorter events, 211.5 us)
Async XLA Ops:
  7.2 274.5 %copy-start = (bf16[512,2048]{1,0:T(8,128)(2,1)S(1)}, bf16[512,2048]{1,0:T(8,128)(2,1)}, u32[]{:S(2)}) copy-start(bf16[512,2048]{1,0:T(8,128)(2,1)} %param.47) | copy-start | bytes 6291460
  7.2 12.1 %copy-start.2 = (bf16[2,512,512]{2,1,0:T(8,128)(2,1)S(1)}, bf16[2,512,512]{2,1,0:T(8,128)(2,1)}, u32[]{:S(2)}) copy-start(bf16[2,512,512]{2,1,0:T(8,128)(2,1)} %param.32) | copy-start | bytes 3145732
  7.2 10.6 %copy-start.48 = (f32[512]{0:T(512)S(1)}, f32[512]{0:T(512)}, u32[]{:S(2)}) copy-start(f32[512]{0:T(512)} %param.38) | copy-start | bytes 6148
  7.2 10.6 %copy-start.63 = (f32[512]{0:T(512)S(1)}, f32[512]{0:T(512)}, u32[]{:S(2)}) copy-start(f32[512]{0:T(512)} %param.39) | copy-start | bytes 6148
  7.2 100.6 %all-gather.2.cloned.1.call-start = ((), (), s32[]{:S(2)}) async-start(), calls=%async_computation.1 | async-start | bytes 9437184 | tf_op jit(solution)/shard_map/all_gather | solution.py:85
  8.6 11.1 %copy-start.56 = (f32[2,256]{1,0:T(2,128)}, f32[2,256]{1,0:T(2,128)S(1)}, u32[]{:S(2)}) copy-start(f32[2,256]{1,0:T(2,128)S(1)} %broadcast_multiply_fusion.2) | copy-start | bytes 6148
  10.0 9.8 %copy-start.61 = (f32[2,256]{1,0:T(2,128)}, f32[2,256]{1,0:T(2,128)S(1)}, u32[]{:S(2)}) copy-start(f32[2,256]{1,0:T(2,128)S(1)} %add_rsqrt_fusion) | copy-start | bytes 6148
  11.5 8.3 copy-start.38
  13.7 10.8 %copy-start.44 = (f32[2,512]{1,0:T(2,128)}, f32[2,512]{1,0:T(2,128)S(1)}, u32[]{:S(2)}) copy-start(f32[2,512]{1,0:T(2,128)S(1)} %fusion.125) | copy-start | bytes 12292
  17.9 3.2 copy-start.32
  17.9 3.2 copy-start.34
  24.5 6.9 copy-start.28
  24.6 647.1 %reduce-scatter.2.cloned.1.call-start = ((), (), s32[]{:S(2)}) async-start(), calls=%async_computation.2 | async-start | bytes 9437184 | tf_op jit(solution)/shard_map/reduce_scatter | solution.py:296
  160.9 6.7 copy-start.8
  176.6 6.7 copy-start.8
  244.9 6.7 copy-start.8
  260.6 6.7 copy-start.8
  278.7 3.0 copy-start.46
  278.7 3.0 copy-start.54
  281.2 35.2 %copy-start.4 = (f32[2,512,512]{2,1,0:T(8,128)}, f32[2,512,512]{2,1,0:T(8,128)S(1)}, u32[]{:S(2)}) copy-start(f32[2,512,512]{2,1,0:T(8,128)S(1)} %get-tuple-element.1057) | copy-start | bytes 6291460
  281.2 35.2 %copy-start.40 = (f32[2,512]{1,0:T(2,128)}, f32[2,512]{1,0:T(2,128)S(1)}, u32[]{:S(2)}) copy-start(f32[2,512]{1,0:T(2,128)S(1)} %broadcast_multiply_fusion) | copy-start | bytes 12292
  281.7 34.7 %copy-start.42 = (f32[2,512]{1,0:T(2,128)}, f32[2,512]{1,0:T(2,128)S(1)}, u32[]{:S(2)}) copy-start(f32[2,512]{1,0:T(2,128)S(1)} %fusion.126) | copy-start | bytes 12292
  285.9 20.2 %copy-start.23 = (bf16[2,512,512]{2,1,0:T(8,128)(2,1)S(1)}, bf16[2,512,512]{2,1,0:T(8,128)(2,1)}, u32[]{:S(2)}) copy-start(bf16[2,512,512]{2,1,0:T(8,128)(2,1)} %param.49) | copy-start | bytes 3145732
  285.9 20.2 %copy-start.72 = (bf16[2048,512]{1,0:T(8,128)(2,1)S(1)}, bf16[2048,512]{1,0:T(8,128)(2,1)}, u32[]{:S(2)}) copy-start(bf16[2048,512]{1,0:T(8,128)(2,1)} %param.48) | copy-start | bytes 6291460
  312.9 3.4 copy-start.15
  317.2 3.1 copy-start.10
  317.3 3.1 copy-start.50
  318.7 2.2 copy-start.25
  376.2 23.1 %copy-start.67 = (f32[2,8]{1,0:T(2,128)S(1)}, f32[2,8]{1,0:T(2,128)}, u32[]{:S(2)}) copy-start(f32[2,8]{1,0:T(2,128)} %get-tuple-element.1969) | copy-start | bytes 196 | tf_op jit(solution)/shard_map/while
  376.2 23.1 %copy-start.58 = (f32[2,8,512]{2,1,0:T(8,128)S(1)}, f32[2,8,512]{2,1,0:T(8,128)}, u32[]{:S(2)}) copy-start(f32[2,8,512]{2,1,0:T(8,128)} %get-tuple-element.1968) | copy-start | bytes 98308 | tf_op jit(solution)/shard_map/while
  453.6 23.1 %copy-start.67 = (f32[2,8]{1,0:T(2,128)S(1)}, f32[2,8]{1,0:T(2,128)}, u32[]{:S(2)}) copy-start(f32[2,8]{1,0:T(2,128)} %get-tuple-element.1969) | copy-start | bytes 196 | tf_op jit(solution)/shard_map/while
  453.6 23.1 %copy-start.58 = (f32[2,8,512]{2,1,0:T(8,128)S(1)}, f32[2,8,512]{2,1,0:T(8,128)}, u32[]{:S(2)}) copy-start(f32[2,8,512]{2,1,0:T(8,128)} %get-tuple-element.1968) | copy-start | bytes 98308 | tf_op jit(solution)/shard_map/while
  485.4 11.3 %copy-start.60 = (f32[2,8,512]{2,1,0:T(8,128)S(1)}, f32[2,8,512]{2,1,0:T(8,128)}, u32[]{:S(2)}) copy-start(f32[2,8,512]{2,1,0:T(8,128)} %get-tuple-element.2054) | copy-start | bytes 98308 | tf_op jit(solution)/shard_map/while
  515.8 13.2 %copy-start.7 = (bf16[2,8,768,64]{2,3,1,0:T(8,128)(2,1)S(1)}, bf16[2,8,768,64]{2,3,1,0:T(8,128)(2,1)}, u32[]{:S(2)}) copy-start(bf16[2,8,768,64]{2,3,1,0:T(8,128)(2,1)} %fusion.216) | copy-start | bytes 4718596 | tf_op jit(solution)/shard_map/while
  543.7 11.3 %copy-start.60 = (f32[2,8,512]{2,1,0:T(8,128)S(1)}, f32[2,8,512]{2,1,0:T(8,128)}, u32[]{:S(2)}) copy-start(f32[2,8,512]{2,1,0:T(8,128)} %get-tuple-element.2054) | copy-start | bytes 98308 | tf_op jit(solution)/shard_map/while
  574.0 13.2 %copy-start.7 = (bf16[2,8,768,64]{2,3,1,0:T(8,128)(2,1)S(1)}, bf16[2,8,768,64]{2,3,1,0:T(8,128)(2,1)}, u32[]{:S(2)}) copy-start(bf16[2,8,768,64]{2,3,1,0:T(8,128)(2,1)} %fusion.216) | copy-start | bytes 4718596 | tf_op jit(solution)/shard_map/while
  594.5 3.2 copy-start.20
  594.5 323.4 %all-reduce.4.cloned.1.call-start = ((), (), s32[]{:S(2)}) async-start(), calls=%async_computation.3 | async-start | bytes 25165824 | tf_op jit(solution)/shard_map/psum | solution.py:328
  596.0 4.9 copy-start.22
  596.0 4.9 copy-start.24
  600.9 4.5 copy-start.5
  600.9 4.5 copy-start.16
  600.9 4.5 copy-start.41
  600.9 4.5 copy-start.43
  600.9 4.5 copy-start.47
  600.9 4.5 copy-start.55
  678.1 6.3 copy-start.33
  678.1 6.3 copy-start.35
  678.1 6.3 copy-start.71
  684.4 1.9 copy-start.17
  684.4 2.1 copy-start.3
  684.4 2.1 copy-start.31
  684.4 2.1 copy-start.39
  684.5 2.1 copy-start.49
  686.6 2.6 copy-start.45
  687.9 2.5 copy-start.65
  687.9 2.5 copy-start.66
  687.9 43.6 %copy-start.11 = (f32[2,512,512]{2,1,0:T(8,128)S(1)}, f32[2,512,512]{2,1,0:T(8,128)}, u32[]{:S(2)}) copy-start(f32[2,512,512]{2,1,0:T(8,128)} %copy-done.10) | copy-start | bytes 6291460
  687.9 43.6 %copy-start.51 = (f32[2,512]{1,0:T(2,128)S(1)}, f32[2,512]{1,0:T(2,128)}, u32[]{:S(2)}) copy-start(f32[2,512]{1,0:T(2,128)} %copy-done.50) | copy-start | bytes 12292
  917.9 4.8 copy-start.30
  917.9 5.8 copy-start.29
  920.3 4.4 copy-start.19
  924.7 3.7 copy-start.18
  924.7 5.7 copy-start.1
  (34 other events, 45.9 us)
Sparse Core Ops, SparseCore 0:
  24.7 83.0 all-gather.1
  594.6 77.0 reduce-scatter.1
  680.4 237.4 all-reduce.3
where the time goes:
time: 945 us; the launch traced here: 937 us
  waiting for transfers between devices  318 us (34%)
  matrix products  271 us (29%)
  local copies, waits for them, and re-layouts  199 us (21%)
  other arithmetic  75.8 us (8%)
  blocking collectives  46.4 us (5%)
  between operations  14.8 us (2%)
  loops' own time  11.7 us (1%)
    psum x1, waiting for transfers between devices, per_device(): lax.psum((grad_first_g, grad_first_b, grad_query_w, grad_key_w, grad_valu...  183 us
    all_gather x1, waiting for transfers between devices, per_device(): lax.all_gather(key_value, 'blk', axis=0, tiled=True)  73.6 us
    reduce_scatter x1, waiting for transfers between devices, per_device(): lax.psum_scatter(pieces.reshape(lax.axis_size('blk') * key_rows, seq_coun...  61.7 us
    dot_general x14, matrix products, block_scores(): jnp.einsum('qhd,khd->hqk', q_heads, key_block, preferred_element_type=jnp...  58.7 us
    dot_general x8, matrix products, probs_of(): jnp.einsum('qhd,khd->hqk', d_heads, value_block, preferred_element_type=j...  57.9 us
    psum x1, blocking collectives, per_device(): lax.psum((grad_first_g, grad_first_b, grad_query_w, grad_key_w, grad_valu...  41 us
    dot_general x2, matrix products, pair_terms(): jnp.einsum('hqk,qhd->khd', d_scores, q_heads, preferred_element_type=jnp....  38 us
    dot_general x4, matrix products, out_step(): jnp.einsum('hqk,khd->qhd', attn_probs, pieces[3], preferred_element_type=...  32.2 us
  transfers between devices with their start and end apart: 3, of which 3 were waited for; matrix products, arithmetic and copies ran while one was open for 3% of the time, Pallas kernels for 0%

commit v1 on v0

--- a/solution.py
+++ b/solution.py
@@ -326,20 +326,23 @@
     grad_first_g = gain_slots + gain_mem
     grad_first_b = shift_slots + shift_mem
     summed = lax.psum(
-        (
-            grad_first_g,
-            grad_first_b,
-            grad_query_w,
-            grad_key_w,
-            grad_value_w,
-            grad_out_w,
-            grad_slopes,
-            grad_second_g,
-            grad_second_b,
-            grad_hidden_w,
-            grad_output_w,
+        lax.psum(
+            (
+                grad_first_g,
+                grad_first_b,
+                grad_query_w,
+                grad_key_w,
+                grad_value_w,
+                grad_out_w,
+                grad_slopes,
+                grad_second_g,
+                grad_second_b,
+                grad_hidden_w,
+                grad_output_w,
+            ),
+            "blk",
         ),
-        ("seq", "blk"),
+        "seq",
     )
     return (
         layer_out,

time: 945 us -> 1240 us (1.31)
  waiting for transfers between devices: 318 us -> 611 us
    psum x0 -> x1, waiting for transfers between devices: none -> 184 us  [per_device(): lax.psum(lax.psum((grad_first_g, grad_first_b, grad_query_w, grad_key_w,...]
    psum x1, waiting for transfers between devices: 183 us -> 292 us  [per_device(): lax.psum((grad_first_g, grad_first_b, grad_query_w, grad_key_w, grad_valu...]
    psum x0 -> x1, blocking collectives: none -> 37.4 us  [per_device(): lax.psum(lax.psum((grad_first_g, grad_first_b, grad_query_w, grad_key_w,...]
    psum x1, blocking collectives: 41 us -> 5.06 us  [per_device(): lax.psum((grad_first_g, grad_first_b, grad_query_w, grad_key_w, grad_valu...]
  transfers between devices with their start and end apart: 3 -> 4, of which waited for: 3 -> 4; matrix products, arithmetic and copies ran while one was open for 3% -> 3% of each run, Pallas kernels for 0% -> 0%
where the time goes in v1:
time: 1240 us; the launch traced here: 1230 us
  waiting for transfers between devices  611 us (49%)
  matrix products  271 us (22%)
  local copies, waits for them, and re-layouts  199 us (16%)
  other arithmetic  75.8 us (6%)
  blocking collectives  47.8 us (4%)
  between operations  14.8 us (1%)
    psum x1, waiting for transfers between devices, per_device(): lax.psum((grad_first_g, grad_first_b, grad_query_w, grad_key_w, grad_valu...  292 us
    psum x1, waiting for transfers between devices, per_device(): lax.psum(lax.psum((grad_first_g, grad_first_b, grad_query_w, grad_key_w,...  184 us
    all_gather x1, waiting for transfers between devices, per_device(): lax.all_gather(key_value, 'blk', axis=0, tiled=True)  73.6 us
    reduce_scatter x1, waiting for transfers between devices, per_device(): lax.psum_scatter(pieces.reshape(lax.axis_size('blk') * key_rows, seq_coun...  61.7 us
    dot_general x14, matrix products, block_scores(): jnp.einsum('qhd,khd->hqk', q_heads, key_block, preferred_element_type=jnp...  58.7 us
    dot_general x8, matrix products, probs_of(): jnp.einsum('qhd,khd->hqk', d_heads, value_block, preferred_element_type=j...  57.9 us
    dot_general x2, matrix products, pair_terms(): jnp.einsum('hqk,qhd->khd', d_scores, q_heads, preferred_element_type=jnp....  38 us
    psum x1, blocking collectives, per_device(): lax.psum(lax.psum((grad_first_g, grad_first_b, grad_query_w, grad_key_w,...  37.4 us
  transfers between devices with their start and end apart: 4, of which 4 were waited for; matrix products, arithmetic and copies ran while one was open for 3% of the time, Pallas kernels for 0%

profile of v1, /device:TPU:0, one launch (start us, length us, event | category | flops | bytes accessed | tf_op | source)
XLA Modules:
  0.0 1231.6 jit_solution(710226211708778304)
XLA Ops:
  26.0 5.4 all_gather.7
  34.2 73.6 %all-gather.2.cloned.1.call-done = bf16[1536,2,1024]{0,2,1:T(8,128)(2,1)} async-done(((bf16[768,2,1024]{0,2,1:T(8,128)(2,1)}), bf16[1536,2,1024]{0,2,1:T(8,128)(2,1)}) %all-gather.2.cloned.1.call-update) | async-done | bytes 6291472 | tf_op jit(solution)/shard_map/all_gather | solution.py:85
  110.0 168.7 %while.93 = (s32[]{:T(128)}, bf16[2,512,8,64]{1,3,2,0:T(8,128)(2,1)}, f32[2,8,512]{2,1,0:T(8,128)}, s32[2]{0:T(128)}, bf16[1536,2,1024]{0,2,1:T(8,128)(2,1)}, /*...) while((s32[]{:T(128)}, ...), condition=%wide.region_11.12_spmd.clone, body=%wide.region_4.11_spmd.clone.sunk | while | flops 1264345600 | bytes 82579288 | solution.py:156
  123.6 4.6 reshape.453
  131.0 4.6 reshape.454
  138.4 21.8 %while.98 = (s32[]{:T(128)}, f32[8,512]{1,0:T(8,128)S(1)}, f32[8,512]{1,0:T(8,128)S(1)}, s32[2,768]{1,0:T(2,128)S(1)}, s32[512]{0:T(512)S(1)}, /*index=5*/bf16[2...) while((s32[]{:T(128)}, f32[8,512]{1,0:T(8,128)S(1)}, ...), condition=%wide.region_8.8_spmd.clone, body=%wide.region_5.7_spmd.clone.sunk | while | flops 438456320 | bytes 32610988 | solution.py:125
  139.6 5.3 fusion.232
  145.0 4.3 exponential_reduce_fusion.2
  150.5 5.3 fusion.232
  155.9 4.3 exponential_reduce_fusion.2
  160.9 31.5 %while.99 = (s32[]{:T(128)}, f32[512,8,64]{0,2,1:T(8,128)}, bf16[2,768,8,64]{1,3,2,0:T(8,128)(2,1)}, s32[2,768]{1,0:T(2,128)S(1)}, s32[512]{0:T(512)S(1)}, /*ind...) while((s32[]{:T(128)}, f32[512,8,64]{0,2,1:T(8,128)}, ...), condition=%wide.region_10.10_spmd.clone, body=%wide.region_9.9_spmd.clone.sunk | while | flops 825884672 | bytes 19438292 | solution.py:151
  163.3 4.3 constant_dynamic-slice_fusion.18
  167.6 8.0 fusion.238
  179.0 4.3 constant_dynamic-slice_fusion.18
  183.4 8.1 fusion.238
  207.6 4.6 reshape.453
  215.0 4.6 reshape.454
  222.5 21.8 %while.98 = (s32[]{:T(128)}, f32[8,512]{1,0:T(8,128)S(1)}, f32[8,512]{1,0:T(8,128)S(1)}, s32[2,768]{1,0:T(2,128)S(1)}, s32[512]{0:T(512)S(1)}, /*index=5*/bf16[2...) while((s32[]{:T(128)}, f32[8,512]{1,0:T(8,128)S(1)}, ...), condition=%wide.region_8.8_spmd.clone, body=%wide.region_5.7_spmd.clone.sunk | while | flops 438456320 | bytes 32610988 | solution.py:125
  223.7 5.3 fusion.232
  229.0 4.3 exponential_reduce_fusion.2
  234.5 5.3 fusion.232
  239.9 4.3 exponential_reduce_fusion.2
  244.9 31.5 %while.99 = (s32[]{:T(128)}, f32[512,8,64]{0,2,1:T(8,128)}, bf16[2,768,8,64]{1,3,2,0:T(8,128)(2,1)}, s32[2,768]{1,0:T(2,128)S(1)}, s32[512]{0:T(512)S(1)}, /*ind...) while((s32[]{:T(128)}, f32[512,8,64]{0,2,1:T(8,128)}, ...), condition=%wide.region_10.10_spmd.clone, body=%wide.region_9.9_spmd.clone.sunk | while | flops 825884672 | bytes 19438292 | solution.py:151
  247.3 4.3 constant_dynamic-slice_fusion.18
  251.6 8.1 fusion.238
  263.1 4.3 constant_dynamic-slice_fusion.18
  267.4 8.1 fusion.238
  281.7 4.2 fusion.108
  286.0 20.1 %multiply_convert_fusion = (bf16[2,512,2048]{2,1,0:T(8,128)(2,1)}, f32[2,512,2048]{2,1,0:T(8,128)}) fusion(f32[2,512,2048]{2,1,0:T(8,128)S(1)} %get-tuple-element.1069, u8[512,2048]{1,0:T(8,128)(4,1)S(1)} %get-tuple-element.841, u8[512,2048]{1,0:T(8,128)(4,1)S(1)} %get-tuple-element.840), kind=kLoop, calls=%fused_computation.134 | loop fusion | flops 146800640 | bytes 23068672 | tf_op jit(solution)/shard_map/convert_element_type | solution.py:165
  306.1 6.8 add_convert_fusion
  322.6 155.2 %while.96 = (s32[]{:T(128)}, bf16[2,512,8,64]{1,3,2,0:T(8,128)(2,1)}, f32[2,8,512]{2,1,0:T(8,128)}, f32[2,8]{1,0:T(2,128)}, s32[2]{0:T(128)}, /*index=5*/bf16[15...) while((s32[]{:T(128)}, ...), condition=%wide.region_23.24_spmd.clone, body=%wide.region_16.23_spmd.clone.sunk | while | flops 2073039360 | bytes 125587736 | solution.py:248
  334.2 4.7 copy.151
  348.6 5.2 reshape.456
  353.7 4.4 copy.153
  358.2 18.1 %while.100 = (s32[]{:T(128)}, f32[8,512]{1,0:T(8,128)S(1)}, s32[2,768]{1,0:T(2,128)S(1)}, s32[512]{0:T(512)S(1)}, bf16[2,768,8,64]{1,3,2,0:T(8,128)(2,1)S(1)}, /...) while((s32[]{:T(128)}, f32[8,512]{1,0:T(8,128)S(1)}, ...), condition=%wide.region_19.19_spmd.clone, body=%wide.region_17.18_spmd.clone.sunk | while | flops 828510208 | bytes 40212728 | solution.py:222
  360.5 6.6 fusion.222
  369.6 6.6 fusion.222
  376.3 23.0 %while.101 = (s32[]{:T(128)}, f32[512,8,64]{0,2,1:T(8,128)S(1)}, f32[8]{0:T(128)S(1)}, bf16[2,768,8,64]{1,3,2,0:T(8,128)(2,1)S(1)}, s32[2,768]{1,0:T(2,128)S(1)}...) while((s32[]{:T(128)}, f32[512,8,64]{0,2,1:T(8,128)S(1)}, ...), condition=%wide.region_22.22_spmd.clone, body=%wide.region_20.21_spmd.clone.sunk | while | flops 1244266496 | bytes 49339216 | solution.py:243
  378.6 7.8 multiply_reduce_fusion.5
  390.1 7.8 multiply_reduce_fusion.5
  411.6 4.7 copy.151
  425.9 5.2 reshape.456
  431.1 4.4 copy.153
  435.5 18.1 %while.100 = (s32[]{:T(128)}, f32[8,512]{1,0:T(8,128)S(1)}, s32[2,768]{1,0:T(2,128)S(1)}, s32[512]{0:T(512)S(1)}, bf16[2,768,8,64]{1,3,2,0:T(8,128)(2,1)S(1)}, /...) while((s32[]{:T(128)}, f32[8,512]{1,0:T(8,128)S(1)}, ...), condition=%wide.region_19.19_spmd.clone, body=%wide.region_17.18_spmd.clone.sunk | while | flops 828510208 | bytes 40212728 | solution.py:222
  437.9 6.6 fusion.222
  446.9 6.6 fusion.222
  453.6 23.0 %while.101 = (s32[]{:T(128)}, f32[512,8,64]{0,2,1:T(8,128)S(1)}, f32[8]{0:T(128)S(1)}, bf16[2,768,8,64]{1,3,2,0:T(8,128)(2,1)S(1)}, s32[2,768]{1,0:T(2,128)S(1)}...) while((s32[]{:T(128)}, f32[512,8,64]{0,2,1:T(8,128)S(1)}, ...), condition=%wide.region_22.22_spmd.clone, body=%wide.region_20.21_spmd.clone.sunk | while | flops 1244266496 | bytes 49339216 | solution.py:243
  456.0 7.8 multiply_reduce_fusion.5
  467.5 7.8 multiply_reduce_fusion.5
  477.8 116.6 %while.97 = (s32[]{:T(128)}, bf16[2,768,2,1024]{3,1,0,2:T(8,128)(2,1)}, s32[2]{0:T(128)S(1)}, s32[2,2,1536]{2,1,0:T(2,128)}, bf16[1536,2,1024]{0,2,1:T(8,128)(2,...) while((s32[]{:T(128)}, ...), condition=%wide.region_25.26_spmd.clone, body=%wide.region_24.25_spmd.clone.sunk | while | flops 3319529984 | bytes 129511832 | solution.py:295
  485.4 11.3 fusion.214
  496.8 19.0 %fusion.216 = bf16[2,8,768,64]{2,3,1,0:T(8,128)(2,1)} fusion(bf16[2,512,8,64]{1,3,2,0:T(8,128)(2,1)} %get-tuple-element.2060, f32[2,8,768,512]{3,2,1,0:T(8,128)} %fusion.214, f32[2,8,512]{2,1,0:T(8,128)S(1)} %copy-done.60, f32[2,8,512]{2,1,0:T(8,128)} %get-tuple-element.2063, f32[2,512,768]{1,2,0:T(8,128)S(1)} %subtract_convert_fusion.10, ...), kind=kOutput, calls=%fused_computation.15.clone.1 | convolution fusion | flops 1662517248 | bytes 34406432 | tf_op jit(solution)/shard_map/while/body/eval_jaxpr/vmap(hqk,qhd->khd)/dot_general | solution.py:272
  515.8 13.2 %fusion.215 = bf16[2,8,768,64]{2,3,1,0:T(8,128)(2,1)S(1)} fusion(bf16[2,512,8,64]{1,3,2,0:T(8,128)(2,1)} %get-tuple-element.2064, f32[2,8,768,512]{3,2,1,0:T(8,128)} %fusion.214, f32[2,8,512]{2,1,0:T(8,128)} %get-tuple-element.2063, f32[2,512,768]{1,2,0:T(8,128)S(1)} %subtract_convert_fusion.10, f32[8]{0:T(128)} %get-tuple-element.2061, ...), kind=kOutput, calls=%fused_computation.10.clone.1 | convolution fusion | flops 843055104 | bytes 31752224 | tf_op jit(solution)/shard_map/while/body/eval_jaxpr/vmap(hqk,qhd->khd)/dot_general | solution.py:265
  543.7 11.3 fusion.214
  555.0 19.0 %fusion.216 = bf16[2,8,768,64]{2,3,1,0:T(8,128)(2,1)} fusion(bf16[2,512,8,64]{1,3,2,0:T(8,128)(2,1)} %get-tuple-element.2060, f32[2,8,768,512]{3,2,1,0:T(8,128)} %fusion.214, f32[2,8,512]{2,1,0:T(8,128)S(1)} %copy-done.60, f32[2,8,512]{2,1,0:T(8,128)} %get-tuple-element.2063, f32[2,512,768]{1,2,0:T(8,128)S(1)} %subtract_convert_fusion.10, ...), kind=kOutput, calls=%fused_computation.15.clone.1 | convolution fusion | flops 1662517248 | bytes 34406432 | tf_op jit(solution)/shard_map/while/body/eval_jaxpr/vmap(hqk,qhd->khd)/dot_general | solution.py:272
  574.0 13.2 %fusion.215 = bf16[2,8,768,64]{2,3,1,0:T(8,128)(2,1)S(1)} fusion(bf16[2,512,8,64]{1,3,2,0:T(8,128)(2,1)} %get-tuple-element.2064, f32[2,8,768,512]{3,2,1,0:T(8,128)} %fusion.214, f32[2,8,512]{2,1,0:T(8,128)} %get-tuple-element.2063, f32[2,512,768]{1,2,0:T(8,128)S(1)} %subtract_convert_fusion.10, f32[8]{0:T(128)} %get-tuple-element.2061, ...), kind=kOutput, calls=%fused_computation.10.clone.1 | convolution fusion | flops 843055104 | bytes 31752224 | tf_op jit(solution)/shard_map/while/body/eval_jaxpr/vmap(hqk,qhd->khd)/dot_general | solution.py:265
  600.9 4.4 convolution_bitcast_fusion.1
  605.4 4.7 convolution_bitcast_fusion.2
  610.0 61.7 %reduce-scatter.2.cloned.1.call-done = bf16[768,2,1024]{2,0,1:T(8,128)(2,1)} async-done(((bf16[1536,2,1024]{2,0,1:T(8,128)(2,1)}), bf16[768,2,1024]{2,0,1:T(8,128)(2,1)}) %reduce-scatter.2.cloned.1.call-update) | async-done | bytes 3145744 | tf_op jit(solution)/shard_map/reduce_scatter | solution.py:296
  677.4 291.6 %all-reduce.9.cloned.1.call-done = (f32[512,512]{1,0:T(8,128)}, f32[512,512]{1,0:T(8,128)}, f32[512,512]{1,0:T(8,128)}, f32[512,512]{1,0:T(8,128)}, f32[512,2048]{1,0:T(8,128)}, /*index=5*/f32[2048,512]{1,0:T(8,128)}) async-done(((f32[512,512]{1,0:T(8,128)}, f32[512,512]{1,0:T(8,128)}, f32[512,512]{1,0:T(8,128)}, f32[512,512]{1,0:T(8,128)}, f32[512,2048]{1,0:T(8,128)}, /*index=5*/f32[2048,512]{1,0:T(8,128)}), ...) | async-done | bytes 12582928 | tf_op jit(solution)/shard_map/psum | solution.py:329
  969.8 6.3 add_convert_fusion.2
  982.2 5.1 all-reduce.2
  987.2 37.4 %all-reduce = (f32[512]{0:T(512)}, f32[512]{0:T(512)}, f32[8]{0:T(128)}, f32[512]{0:T(512)}, f32[512]{0:T(512)}) all-reduce(f32[512]{0:T(512)S(1)} %get-tuple-element.1026, f32[512]{0:T(512)S(1)} %get-tuple-element.1027, f32[8]{0:T(128)S(1)} %get-tuple-element.1028, ...), channel_id=1, replica_groups=mesh['seq'=16,'blk'=2] {'seq'}, use_global_device_ids=true, to_apply=%region_32.33 | all-reduce | flops 2056 | bytes 16448 | tf_op jit(solution)/shard_map/psum | solution.py:328
  1027.9 184.5 %all-reduce.7.cloned.1.call-done = (f32[512,512]{1,0:T(8,128)}, f32[512,512]{1,0:T(8,128)}, f32[512,512]{1,0:T(8,128)}, f32[512,512]{1,0:T(8,128)}, f32[512,2048]{1,0:T(8,128)}, /*index=5*/f32[2048,512]{1,0:T(8,128)}) async-done(((f32[512,512]{1,0:T(8,128)}, f32[512,512]{1,0:T(8,128)}, f32[512,512]{1,0:T(8,128)}, f32[512,512]{1,0:T(8,128)}, f32[512,2048]{1,0:T(8,128)}, /*index=5*/f32[2048,512]{1,0:T(8,128)}), ...) | async-done | bytes 12582928 | tf_op jit(solution)/shard_map/psum | solution.py:328
  (428 shorter events, 219.5 us)
Async XLA Ops:
  7.2 274.5 %copy-start = (bf16[512,2048]{1,0:T(8,128)(2,1)S(1)}, bf16[512,2048]{1,0:T(8,128)(2,1)}, u32[]{:S(2)}) copy-start(bf16[512,2048]{1,0:T(8,128)(2,1)} %param.47) | copy-start | bytes 6291460
  7.2 12.1 copy-start.2
  7.2 10.6 copy-start.48
  7.2 10.6 copy-start.63
  7.2 100.6 %all-gather.2.cloned.1.call-start = ((), (), s32[]{:S(2)}) async-start(), calls=%async_computation.1 | async-start | bytes 9437184 | tf_op jit(solution)/shard_map/all_gather | solution.py:85
  8.6 11.1 copy-start.56
  10.0 9.8 copy-start.61
  11.5 8.3 copy-start.38
  13.7 10.8 copy-start.44
  17.9 3.2 copy-start.32
  17.9 3.2 copy-start.34
  24.5 6.9 copy-start.28
  24.6 647.1 %reduce-scatter.2.cloned.1.call-start = ((), (), s32[]{:S(2)}) async-start(), calls=%async_computation.2 | async-start | bytes 9437184 | tf_op jit(solution)/shard_map/reduce_scatter | solution.py:296
  160.9 6.7 copy-start.8
  176.6 6.7 copy-start.8
  244.9 6.7 copy-start.8
  260.6 6.7 copy-start.8
  278.7 3.0 copy-start.46
  278.7 3.0 copy-start.54
  281.2 35.2 %copy-start.4 = (f32[2,512,512]{2,1,0:T(8,128)}, f32[2,512,512]{2,1,0:T(8,128)S(1)}, u32[]{:S(2)}) copy-start(f32[2,512,512]{2,1,0:T(8,128)S(1)} %get-tuple-element.1068) | copy-start | bytes 6291460
  281.2 35.2 %copy-start.40 = (f32[2,512]{1,0:T(2,128)}, f32[2,512]{1,0:T(2,128)S(1)}, u32[]{:S(2)}) copy-start(f32[2,512]{1,0:T(2,128)S(1)} %broadcast_multiply_fusion) | copy-start | bytes 12292
  281.7 34.7 %copy-start.42 = (f32[2,512]{1,0:T(2,128)}, f32[2,512]{1,0:T(2,128)S(1)}, u32[]{:S(2)}) copy-start(f32[2,512]{1,0:T(2,128)S(1)} %fusion.126) | copy-start | bytes 12292
  285.9 20.2 %copy-start.23 = (bf16[2,512,512]{2,1,0:T(8,128)(2,1)S(1)}, bf16[2,512,512]{2,1,0:T(8,128)(2,1)}, u32[]{:S(2)}) copy-start(bf16[2,512,512]{2,1,0:T(8,128)(2,1)} %param.49) | copy-start | bytes 3145732
  285.9 20.2 %copy-start.72 = (bf16[2048,512]{1,0:T(8,128)(2,1)S(1)}, bf16[2048,512]{1,0:T(8,128)(2,1)}, u32[]{:S(2)}) copy-start(bf16[2048,512]{1,0:T(8,128)(2,1)} %param.48) | copy-start | bytes 6291460
  312.9 3.4 copy-start.15
  317.2 3.1 copy-start.10
  317.3 3.1 copy-start.50
  318.7 2.2 copy-start.25
  376.2 23.1 %copy-start.67 = (f32[2,8]{1,0:T(2,128)S(1)}, f32[2,8]{1,0:T(2,128)}, u32[]{:S(2)}) copy-start(f32[2,8]{1,0:T(2,128)} %get-tuple-element.1980) | copy-start | bytes 196 | tf_op jit(solution)/shard_map/while
  376.2 23.1 %copy-start.58 = (f32[2,8,512]{2,1,0:T(8,128)S(1)}, f32[2,8,512]{2,1,0:T(8,128)}, u32[]{:S(2)}) copy-start(f32[2,8,512]{2,1,0:T(8,128)} %get-tuple-element.1979) | copy-start | bytes 98308 | tf_op jit(solution)/shard_map/while
  453.6 23.1 %copy-start.67 = (f32[2,8]{1,0:T(2,128)S(1)}, f32[2,8]{1,0:T(2,128)}, u32[]{:S(2)}) copy-start(f32[2,8]{1,0:T(2,128)} %get-tuple-element.1980) | copy-start | bytes 196 | tf_op jit(solution)/shard_map/while
  453.6 23.1 %copy-start.58 = (f32[2,8,512]{2,1,0:T(8,128)S(1)}, f32[2,8,512]{2,1,0:T(8,128)}, u32[]{:S(2)}) copy-start(f32[2,8,512]{2,1,0:T(8,128)} %get-tuple-element.1979) | copy-start | bytes 98308 | tf_op jit(solution)/shard_map/while
  485.4 11.3 copy-start.60
  515.8 13.2 %copy-start.7 = (bf16[2,8,768,64]{2,3,1,0:T(8,128)(2,1)S(1)}, bf16[2,8,768,64]{2,3,1,0:T(8,128)(2,1)}, u32[]{:S(2)}) copy-start(bf16[2,8,768,64]{2,3,1,0:T(8,128)(2,1)} %fusion.216) | copy-start | bytes 4718596 | tf_op jit(solution)/shard_map/while
  543.7 11.3 copy-start.60
  574.0 13.2 %copy-start.7 = (bf16[2,8,768,64]{2,3,1,0:T(8,128)(2,1)S(1)}, bf16[2,8,768,64]{2,3,1,0:T(8,128)(2,1)}, u32[]{:S(2)}) copy-start(bf16[2,8,768,64]{2,3,1,0:T(8,128)(2,1)} %fusion.216) | copy-start | bytes 4718596 | tf_op jit(solution)/shard_map/while
  594.5 3.2 copy-start.20
  594.5 374.6 %all-reduce.9.cloned.1.call-start = ((), (), s32[]{:S(2)}) async-start(), calls=%async_computation.4 | async-start | bytes 25165824 | tf_op jit(solution)/shard_map/psum | solution.py:329
  596.0 4.9 copy-start.22
  596.0 4.9 copy-start.24
  600.9 4.5 copy-start.5
  600.9 4.5 copy-start.16
  600.9 4.5 copy-start.41
  600.9 4.5 copy-start.43
  600.9 4.5 copy-start.47
  600.9 4.5 copy-start.55
  677.4 535.0 %all-reduce.7.cloned.1.call-start = ((), (), s32[]{:S(2)}) async-start(), calls=%async_computation.3 | async-start | bytes 25165824 | tf_op jit(solution)/shard_map/psum | solution.py:328
  969.8 6.3 copy-start.33
  969.8 6.3 copy-start.35
  969.8 6.3 copy-start.71
  976.1 2.2 copy-start.3
  976.1 2.1 copy-start.31
  976.1 2.1 copy-start.39
  976.2 2.1 copy-start.49
  978.3 2.6 copy-start.45
  979.6 2.5 copy-start.65
  979.6 2.5 copy-start.66
  979.6 45.0 %copy-start.11 = (f32[2,512,512]{2,1,0:T(8,128)S(1)}, f32[2,512,512]{2,1,0:T(8,128)}, u32[]{:S(2)}) copy-start(f32[2,512,512]{2,1,0:T(8,128)} %copy-done.10) | copy-start | bytes 6291460
  979.7 45.0 %copy-start.51 = (f32[2,512]{1,0:T(2,128)S(1)}, f32[2,512]{1,0:T(2,128)}, u32[]{:S(2)}) copy-start(f32[2,512]{1,0:T(2,128)} %copy-done.50) | copy-start | bytes 12292
  1212.4 4.8 copy-start.30
  1212.4 5.8 copy-start.29
  1214.8 4.4 copy-start.19
  1219.1 3.7 copy-start.18
  1219.1 5.7 copy-start.1
  (35 other events, 47.8 us)
Sparse Core Ops, SparseCore 0:
  24.7 83.0 all-gather.1
  594.6 77.0 reduce-scatter.1
  677.5 291.5 all-reduce.8
  974.8 237.4 all-reduce.6
